TPU v7x, 32 devices: a whole 2x2x4 slice. The times are simulated.
32 devices in a mesh: dp: 16 (over z, x, core), tensor: 2 (over y).
Axes of the slice: x: 2, y: 2, z: 4, core: 2. Of those that a mesh axis runs over, the one named last changes fastest.
Arguments:
- tokens: bfloat16 [16384, 1024], P('dp'), may hold values from -6 to 6
- lengths: int32 [16, 64], P('dp'), may hold values from 1 to 60, 1024 in all within a row
- w_qkv: bfloat16 [2, 1024, 3, 1024], P(None, None, None, 'tensor'), may hold values from -0.1875 to 0.1875
- w_out: bfloat16 [2, 1024, 1024], P(None, None, 'tensor'), may hold values from -0.5 to 0.5
- w_up: bfloat16 [2, 1024, 2048], P(None, None, 'tensor'), may hold values from -0.1875 to 0.1875
- w_down: bfloat16 [2, 1024, 2048], P(None, None, 'tensor'), may hold values from -0.125 to 0.125
- norm_gain: float32 [2, 2, 1024], replicated, may hold values from 0.5 to 1.5
- norm_bias: float32 [2, 2, 1024], replicated, may hold values from -1 to 1
- cotangent: bfloat16 [16384, 1024], P('dp'), may hold values from -6 to 6
Outputs:
- output: bfloat16 [16384, 1024], P('dp')
- grad_tokens: float32 [16384, 1024], P('dp')
- grad_qkv: float32 [2, 1024, 3, 1024], P(None, 'dp', None, 'tensor')
- grad_out: float32 [2, 1024, 1024], P(None, 'dp', 'tensor')
- grad_up: float32 [2, 1024, 2048], P(None, 'dp', 'tensor')
- grad_down: float32 [2, 1024, 2048], P(None, 'dp', 'tensor')
- grad_gain: float32 [2, 2, 1024], P(None, None, 'dp')
- grad_bias: float32 [2, 2, 1024], P(None, None, 'dp')
Inputs may be any that keep to these rules, and one draw needn't show every extreme that they name: `lengths`: each row sums to 1024, and some item of every row has exactly 60 tokens.
All inputs are finite; a program needn't handle non-finite values.
Results may differ from a plain program's by a relative error of at most 0.025.
Values may be sent and summed in bfloat16 or wider, within the bound.
A program may use at most 192 MiB of HBM per device.

v0:
```python
import jax
import jax.numpy as jnp
from jax import lax
from jax.sharding import PartitionSpec as P

HEAD_DIM = 128


epsilon = 1e-05
masked_score = -1e30


def norm_rows(values, gain, shift):
    center = values - jnp.mean(values, axis=-1, keepdims=True)
    spread = jnp.mean(center * center, axis=-1, keepdims=True)
    return center * lax.rsqrt(spread + epsilon) * gain + shift


def gelu_exact(values):
    return jax.nn.gelu(values, approximate=False)


def contract_last(left, right):
    return lax.dot_general(
        left, right, (((1,), (1,)), ((), ())), preferred_element_type=jnp.float32
    )


def contract_first(left, right):
    return lax.dot_general(
        left, right, (((0,), (0,)), ((), ())), preferred_element_type=jnp.float32
    )


def windows(values, tile, fill):
    rows = values.shape[0]
    count = rows // tile
    front_pad = jnp.full((tile,) + values.shape[1:], fill, values.dtype)
    padded = jnp.concatenate([front_pad, values], axis=0)
    front = padded[:rows].reshape((count, tile) + values.shape[1:])
    back = padded[tile:].reshape((count, tile) + values.shape[1:])
    return jnp.concatenate([front, back], axis=1)


def unwindow(window_grads, tile):
    count = window_grads.shape[0]
    rows = count * tile
    rest = window_grads.shape[2:]
    front = window_grads[:, :tile].reshape((rows,) + rest)
    back = window_grads[:, tile:].reshape((rows,) + rest)
    tail = jnp.zeros((tile,) + rest, window_grads.dtype)
    return back + jnp.concatenate([front[tile:], tail], axis=0)


def block_scores(q_blk, k_win, m_blk, scale):
    scores = jnp.einsum("sqhd,skhd->shqk", q_blk, k_win, preferred_element_type=jnp.float32) * scale
    return jnp.where(m_blk[:, None], scores, masked_score)


def attend_forward(query, k_win, v_win, allowed, block, tile, scale):
    rows, heads, size = query.shape
    count = rows // block
    sub = block // tile
    q_blocks = query.reshape(count, sub, tile, heads, size)
    k_blocks = k_win.reshape(count, sub, 2 * tile, heads, size)
    v_blocks = v_win.reshape(count, sub, 2 * tile, heads, size)
    m_blocks = allowed.reshape(count, sub, tile, 2 * tile)

    def one_block(items):
        q_blk, k_blk, v_blk, m_blk = items
        scores = block_scores(q_blk, k_blk, m_blk, scale)
        top = jnp.max(scores, axis=-1, keepdims=True)
        weights = jnp.exp(scores - top)
        total = jnp.sum(weights, axis=-1, keepdims=True)
        probs = (weights / total).astype(jnp.bfloat16)
        mixed = jnp.einsum("shqk,skhd->sqhd", probs, v_blk, preferred_element_type=jnp.float32)
        return (mixed, (top + jnp.log(total))[..., 0])

    mixed, lse = lax.map(one_block, (q_blocks, k_blocks, v_blocks, m_blocks))
    return (mixed.reshape(query.shape), lse)


def attend_backward(query, k_win, v_win, allowed, lse, grad_mixed, block, tile, scale):
    rows, heads, size = query.shape
    count = rows // block
    sub = block // tile
    q_blocks = query.reshape(count, sub, tile, heads, size)
    k_blocks = k_win.reshape(count, sub, 2 * tile, heads, size)
    v_blocks = v_win.reshape(count, sub, 2 * tile, heads, size)
    m_blocks = allowed.reshape(count, sub, tile, 2 * tile)
    g_blocks = grad_mixed.reshape(count, sub, tile, heads, size)

    def one_block(items):
        q_blk, k_blk, v_blk, m_blk, l_blk, g_blk = items
        scores = block_scores(q_blk, k_blk, m_blk, scale)
        probs = jnp.exp(scores - l_blk[..., None])
        grad_probs = jnp.einsum("sqhd,skhd->shqk", g_blk, v_blk, preferred_element_type=jnp.float32)
        inner = jnp.sum(grad_probs * probs, axis=-1, keepdims=True)
        grad_scores = (probs * (grad_probs - inner)).astype(jnp.bfloat16)
        grad_query = (
            jnp.einsum("shqk,skhd->sqhd", grad_scores, k_blk, preferred_element_type=jnp.float32)
            * scale
        )
        grad_keys = (
            jnp.einsum("shqk,sqhd->skhd", grad_scores, q_blk, preferred_element_type=jnp.float32)
            * scale
        )
        grad_values = jnp.einsum(
            "shqk,sqhd->skhd", probs.astype(jnp.bfloat16), g_blk, preferred_element_type=jnp.float32
        )
        return (grad_query, grad_keys, grad_values)

    grad_query, grad_keys, grad_values = lax.map(
        one_block, (q_blocks, k_blocks, v_blocks, m_blocks, lse, g_blocks)
    )
    tiles = rows // tile
    grad_keys = unwindow(grad_keys.reshape(tiles, 2 * tile, heads, size), tile)
    grad_values = unwindow(grad_values.reshape(tiles, 2 * tile, heads, size), tile)
    return (grad_query.reshape(query.shape), grad_keys, grad_values)


def local(tokens, lengths, w_qkv, w_out, w_up, w_down, norm_gain, norm_bias, cotangent):
    rows, width = tokens.shape
    layers = w_qkv.shape[0]
    cols = w_qkv.shape[3]
    heads = cols // HEAD_DIM
    block = min(512, rows)
    tile = min(128, rows)
    tiles = rows // tile
    scale = HEAD_DIM ** (-0.5)
    ends = jnp.cumsum(lengths[0])
    place = jnp.arange(rows, dtype=jnp.int32)
    segment = jnp.sum((place[:, None] >= ends[None, :]).astype(jnp.int32), axis=1)
    seg_win = windows(segment, tile, -1)
    place_win = windows(place, tile, -1)
    seg_rows = segment.reshape(tiles, tile)
    place_rows = place.reshape(tiles, tile)
    allowed = (seg_rows[:, :, None] == seg_win[:, None, :]) & (
        place_win[:, None, :] <= place_rows[:, :, None]
    )
    stream = tokens.astype(jnp.float32)
    saved = []
    for layer in range(layers):
        normed, norm_pull = jax.vjp(norm_rows, stream, norm_gain[layer, 0], norm_bias[layer, 0])
        normed = normed.astype(jnp.bfloat16)
        qkv_weight = w_qkv[layer].reshape(width, 3 * cols)
        projected = jnp.dot(normed, qkv_weight, preferred_element_type=jnp.float32).astype(
            jnp.bfloat16
        )
        query = projected[:, :cols].reshape(rows, heads, HEAD_DIM)
        keys = projected[:, cols : 2 * cols].reshape(rows, heads, HEAD_DIM)
        values = projected[:, 2 * cols :].reshape(rows, heads, HEAD_DIM)
        k_win = windows(keys, tile, 0)
        v_win = windows(values, tile, 0)
        mixed, lse = attend_forward(query, k_win, v_win, allowed, block, tile, scale)
        mixed = mixed.reshape(rows, cols).astype(jnp.bfloat16)
        branch = lax.psum(contract_last(mixed, w_out[layer]).astype(jnp.bfloat16), "tensor").astype(
            jnp.float32
        )
        stream = stream + branch
        normed_two, norm_pull_two = jax.vjp(
            norm_rows, stream, norm_gain[layer, 1], norm_bias[layer, 1]
        )
        normed_two = normed_two.astype(jnp.bfloat16)
        upward = jnp.dot(normed_two, w_up[layer], preferred_element_type=jnp.float32)
        active, gelu_pull = jax.vjp(gelu_exact, upward)
        active = active.astype(jnp.bfloat16)
        branch_two = lax.psum(
            contract_last(active, w_down[layer]).astype(jnp.bfloat16), "tensor"
        ).astype(jnp.float32)
        stream = stream + branch_two
        saved.append(
            (
                norm_pull,
                normed,
                query,
                k_win,
                v_win,
                lse,
                mixed,
                norm_pull_two,
                normed_two,
                gelu_pull,
                active,
            )
        )
    output = stream.astype(jnp.bfloat16)
    grad = cotangent.astype(jnp.float32)
    layer_parts = [None] * layers
    for layer in reversed(range(layers)):
        (
            norm_pull,
            normed,
            query,
            k_win,
            v_win,
            lse,
            mixed,
            norm_pull_two,
            normed_two,
            gelu_pull,
            active,
        ) = saved[layer]
        upper = grad.astype(jnp.bfloat16)
        grad_active = jnp.dot(upper, w_down[layer], preferred_element_type=jnp.float32)
        grad_down = contract_first(upper, active)
        grad_upward = gelu_pull(grad_active)[0].astype(jnp.bfloat16)
        grad_up = contract_first(normed_two, grad_upward)
        grad_normed_two = lax.psum(
            contract_last(grad_upward, w_up[layer]).astype(jnp.bfloat16), "tensor"
        ).astype(jnp.float32)
        grad_stream, gain_two, shift_two = norm_pull_two(grad_normed_two)
        grad = grad + grad_stream
        lower = grad.astype(jnp.bfloat16)
        grad_mixed = jnp.dot(lower, w_out[layer], preferred_element_type=jnp.float32).astype(
            jnp.bfloat16
        )
        grad_outproj = contract_first(lower, mixed)
        grad_query, grad_keys, grad_values = attend_backward(
            query,
            k_win,
            v_win,
            allowed,
            lse,
            grad_mixed.reshape(rows, heads, HEAD_DIM),
            block,
            tile,
            scale,
        )
        grad_projected = jnp.concatenate(
            [
                grad_query.reshape(rows, cols),
                grad_keys.reshape(rows, cols),
                grad_values.reshape(rows, cols),
            ],
            axis=1,
        ).astype(jnp.bfloat16)
        grad_qkv = contract_first(normed, grad_projected).reshape(width, 3, cols)
        grad_normed = lax.psum(
            contract_last(grad_projected, w_qkv[layer].reshape(width, 3 * cols)).astype(
                jnp.bfloat16
            ),
            "tensor",
        ).astype(jnp.float32)
        grad_stream, gain_one, shift_one = norm_pull(grad_normed)
        grad = grad + grad_stream
        parts = (
            grad_qkv,
            grad_outproj,
            grad_up,
            grad_down,
            jnp.stack([gain_one, gain_two]),
            jnp.stack([shift_one, shift_two]),
        )
        layer_parts[layer] = parts
    stacked = tuple(
        (jnp.stack([layer_parts[index][member] for index in range(layers)]) for member in range(6))
    )
    stacked = (
        lax.psum_scatter(stacked[0], "dp", scatter_dimension=1, tiled=True),
        lax.psum_scatter(stacked[1], "dp", scatter_dimension=1, tiled=True),
        lax.psum_scatter(stacked[2], "dp", scatter_dimension=1, tiled=True),
        lax.psum_scatter(stacked[3], "dp", scatter_dimension=1, tiled=True),
        lax.psum_scatter(stacked[4], "dp", scatter_dimension=2, tiled=True),
        lax.psum_scatter(stacked[5], "dp", scatter_dimension=2, tiled=True),
    )
    return (output, grad, stacked[0], stacked[1], stacked[2], stacked[3], stacked[4], stacked[5])


def solution(mesh):
    placed = (
        P("dp", None),
        P("dp", None),
        P(None, None, None, "tensor"),
        P(None, None, "tensor"),
        P(None, None, "tensor"),
        P(None, None, "tensor"),
        P(),
        P(),
        P("dp", None),
    )
    return jax.shard_map(
        local,
        mesh=mesh,
        in_specs=placed,
        out_specs=(
            P("dp", None),
            P("dp", None),
            P(None, "dp", None, "tensor"),
            P(None, "dp", "tensor"),
            P(None, "dp", "tensor"),
            P(None, "dp", "tensor"),
            P(None, None, "dp"),
            P(None, None, "dp"),
        ),
        check_vma=False,
    )
```

profile of v0, /device:TPU:0, one launch (start us, length us, event | category | flops | bytes accessed | tf_op | source)
XLA Modules:
  0.0 1507.4 jit_solution(13926353916976065757)
XLA Ops:
  13.3 6.3 fusion.180
  19.6 4.8 copy.209
  24.5 5.8 convolution_convert_fusion.1
  46.1 3.1 pad_maximum_fusion.4
  50.8 20.1 %while.52 = (s32[]{:T(128)}, bf16[2,4,128,4,128]{2,4,3,1,0:T(8,128)(2,1)}, f32[2,4,4,128]{3,2,1,0:T(4,128)S(1)}, bf16[2,4,256,4,128]{4,2,1,0,3:T(8,128)(2,1)}, p...) while((s32[]{:T(128)}, ...), condition=%wide.region_7.8_spmd, body=%wide.region_4.7_spmd.sunk | while | flops 274724864 | bytes 31786704 | solution.py:79
  57.2 3.7 fusion.238
  67.3 3.6 fusion.238
  73.2 4.2 convolution_convert_fusion.5
  77.7 65.5 %all-reduce.20.cloned.1.call-done = bf16[1024,1024]{1,0:T(8,128)(2,1)} async-done(((bf16[1024,1024]{1,0:T(8,128)(2,1)}), bf16[1024,1024]{1,0:T(8,128)(2,1)}) %all-reduce.20.cloned.1.call-update) | async-done | bytes 2097168 | tf_op jit(solution)/shard_map/psum | solution.py:157
  146.7 13.4 multiply_convert_fusion.3
  161.4 3.7 fusion.128
  165.6 4.7 copy.210
  170.3 57.9 %all-reduce.22.cloned.1.call-done = bf16[1024,1024]{1,0:T(8,128)(2,1)} async-done(((bf16[1024,1024]{1,0:T(8,128)(2,1)}), bf16[1024,1024]{1,0:T(8,128)(2,1)}) %all-reduce.22.cloned.1.call-update) | async-done | bytes 2097168 | tf_op jit(solution)/shard_map/psum | solution.py:168
  228.2 3.1 fusion.178
  234.7 4.1 convolution_convert_fusion
  250.5 15.9 %while.53 = (s32[]{:T(128)}, bf16[2,4,128,4,128]{2,4,3,1,0:T(8,128)(2,1)}, f32[2,4,4,128]{3,2,1,0:T(4,128)}, bf16[2,4,256,4,128]{4,2,1,0,3:T(8,128)(2,1)}, pred[...) while((s32[]{:T(128)}, ...), condition=%wide.region_17.18_spmd, body=%wide.region_14.17_spmd.sunk | while | flops 274724864 | bytes 23267448 | solution.py:79
  268.1 4.3 convolution_convert_fusion.4
  272.6 62.8 %all-reduce.24.cloned.1.call-done = bf16[1024,1024]{1,0:T(8,128)(2,1)} async-done(((bf16[1024,1024]{1,0:T(8,128)(2,1)}), bf16[1024,1024]{1,0:T(8,128)(2,1)}) %all-reduce.24.cloned.1.call-update) | async-done | bytes 2097168 | tf_op jit(solution)/shard_map/psum | solution.py:157
  335.4 3.3 fusion.177
  339.5 3.0 copy-done.106
  342.5 12.2 multiply_convert_fusion.2
  354.8 4.1 add_convert_fusion.1
  360.2 3.7 fusion.131
  364.0 63.0 %all-reduce.26.cloned.1.call-done = bf16[1024,1024]{1,0:T(8,128)(2,1)} async-done(((bf16[1024,1024]{1,0:T(8,128)(2,1)}), bf16[1024,1024]{1,0:T(8,128)(2,1)}) %all-reduce.26.cloned.1.call-update) | async-done | bytes 2097168 | tf_op jit(solution)/shard_map/psum | solution.py:209
  427.0 4.9 fusion.83
  445.8 44.7 %while.54 = (s32[]{:T(128)}, bf16[2,4,128,4,128]{2,4,3,1,0:T(8,128)(2,1)}, f32[2,4,256,4,128]{4,2,1,0,3:T(8,128)}, f32[2,4,256,4,128]{4,2,1,0,3:T(8,128)}, bf16[...) while((s32[]{:T(128)}, ...), condition=%wide.region_27.28_spmd, body=%wide.region_25.27_spmd.sunk | while | flops 676591616 | bytes 71740656 | solution.py:113
  459.8 3.1 copy.314
  462.9 4.1 constant_dynamic-update-slice_fusion.6
  482.2 3.1 copy.314
  485.3 4.0 constant_dynamic-update-slice_fusion.6
  505.6 4.6 convolution_convert_fusion.3
  510.5 62.9 %all-reduce.28.cloned.1.call-done = bf16[1024,1024]{1,0:T(8,128)(2,1)} async-done(((bf16[1024,1024]{1,0:T(8,128)(2,1)}), bf16[1024,1024]{1,0:T(8,128)(2,1)}) %all-reduce.28.cloned.1.call-update) | async-done | bytes 2097168 | tf_op jit(solution)/shard_map/psum | solution.py:239
  573.3 4.2 convert_reduce_fusion.2
  586.7 3.7 add_convert_fusion
  591.7 3.7 fusion.125
  595.5 6.0 fusion.134
  601.6 57.0 %all-reduce.30.cloned.1.call-done = bf16[1024,1024]{1,0:T(8,128)(2,1)} async-done(((bf16[1024,1024]{1,0:T(8,128)(2,1)}), bf16[1024,1024]{1,0:T(8,128)(2,1)}) %all-reduce.30.cloned.1.call-update) | async-done | bytes 2097168 | tf_op jit(solution)/shard_map/psum | solution.py:209
  658.6 3.9 convert_reduce_fusion.1
  662.5 3.2 fusion.85
  678.6 43.8 %while.55 = (s32[]{:T(128)}, bf16[2,4,128,4,128]{2,4,3,1,0:T(8,128)(2,1)}, f32[2,4,256,4,128]{4,2,1,0,3:T(8,128)}, f32[2,4,256,4,128]{4,2,1,0,3:T(8,128)}, bf16[...) while((s32[]{:T(128)}, ...), condition=%wide.region_36.37_spmd, body=%wide.region_34.36_spmd.sunk | while | flops 676591616 | bytes 71740656 | solution.py:113
  692.0 3.1 copy.319
  695.1 4.1 constant_dynamic-update-slice_fusion.7
  713.9 3.1 copy.319
  717.0 4.1 constant_dynamic-update-slice_fusion.7
  724.3 3.0 slice.192
  737.5 4.6 convolution_convert_fusion.2
  742.8 9.7 fusion.174
  752.6 6.1 fusion.169
  758.7 91.8 %all-reduce.34.cloned.1.call-done = (bf16[1024,1024]{1,0:T(8,128)(2,1)}, bf16[1024,1024]{1,0:T(8,128)(2,1)}) async-done(((bf16[1024,1024]{1,0:T(8,128)(2,1)}, bf16[1024,1024]{1,0:T(8,128)(2,1)}), (bf16[1024,1024]{1,0:T(8,128)(2,1)}, bf16[1024,1024]{1,0:T(8,128)(2,1)})) %all-reduce.34.cloned.1.call-update) | async-done | bytes 4194320 | tf_op jit(solution)/shard_map/psum | solution.py:168
  855.5 3.9 fusion.86
  861.7 12.0 pad_maximum_fusion
  873.7 19.4 %copy.179 = f32[2,1024,3,512]{3,0,2,1:T(2,128)} copy(f32[2,1024,3,512]{1,3,2,0:T(8,128)} %pad_maximum_fusion) | data formatting | bytes 25165824 | tf_op jit(solution)/shard_map/stack | solution.py:257
  893.2 3.3 convolution_bitcast_fusion.8
  900.6 4.9 convolution_bitcast_fusion.4
  907.9 4.1 pad_maximum_fusion.2
  912.8 5.7 convolution_bitcast_fusion.6
  921.5 4.1 pad_maximum_fusion.1
  927.5 5.2 add_convert_fusion.2
  932.6 3.2 add_add_fusion.4
  937.4 33.0 %reduce-scatter.16.cloned.1.call-done = f32[64,4]{1,0:T(8,128)} async-done(((f32[1024,4]{1,0:T(8,128)}), f32[64,4]{1,0:T(8,128)}) %reduce-scatter.16.cloned.1.call-update) | async-done | bytes 1040
  971.9 234.2 %all-reduce.32.cloned.1.call-done = f32[2,1024,3,512]{3,0,2,1:T(2,128)} async-done(((f32[2,1024,3,512]{3,0,2,1:T(2,128)}), f32[2,1024,3,512]{3,0,2,1:T(2,128)}) %all-reduce.32.cloned.1.call-update) | async-done | bytes 12582928
  1208.5 74.9 %reduce-scatter.10.cloned.1.call-done = f32[2,64,512]{2,1,0:T(8,128)} async-done(((f32[2,1024,512]{2,1,0:T(8,128)}), f32[2,64,512]{2,1,0:T(8,128)}) %reduce-scatter.10.cloned.1.call-update) | async-done | bytes 262160 | tf_op jit(solution)/shard_map/reduce_scatter | solution.py:261
  1283.4 108.2 %reduce-scatter.14.cloned.1.call-done = f32[2,64,1024]{2,1,0:T(8,128)} async-done(((f32[2,1024,1024]{2,1,0:T(8,128)}), f32[2,64,1024]{2,1,0:T(8,128)}) %reduce-scatter.14.cloned.1.call-update) | async-done | bytes 524304 | tf_op jit(solution)/shard_map/reduce_scatter | solution.py:263
  1391.6 109.0 %reduce-scatter.12.cloned.1.call-done = f32[2,64,1024]{2,1,0:T(8,128)} async-done(((f32[2,1024,1024]{2,1,0:T(8,128)}), f32[2,64,1024]{2,1,0:T(8,128)}) %reduce-scatter.12.cloned.1.call-update) | async-done | bytes 524304 | tf_op jit(solution)/shard_map/reduce_scatter | solution.py:262
  (481 shorter events, 227.5 us)
Async XLA Ops:
  7.2 5.5 copy-start.94
  7.2 136.0 %all-reduce.20.cloned.1.call-start = ((), (), s32[]{:S(2)}) async-start(), calls=%async_computation.5 | async-start | bytes 4194304 | tf_op jit(solution)/shard_map/psum | solution.py:157
  9.2 15.2 %copy-start.63 = (f32[1024]{0:T(1024)}, f32[1024]{0:T(1024)S(1)}, u32[]{:S(2)}) copy-start(f32[1024]{0:T(1024)S(1)} %broadcast_multiply_fusion.3) | copy-start | bytes 12292
  12.1 12.4 copy-start.85
  12.7 11.7 copy-start.72
  13.3 11.1 copy-start.99
  43.5 5.7 copy-start.103
  73.2 72.4 %copy-start.48 = (bf16[2,4,128,4,128]{4,3,2,1,0:T(4,128)(2,1)}, bf16[2,4,128,4,128]{4,3,2,1,0:T(4,128)(2,1)S(1)}, u32[]{:S(2)}) copy-start(bf16[2,4,128,4,128]{4,3,2,1,0:T(4,128)(2,1)S(1)} %copy.149) | copy-start | bytes 3145732
  77.4 69.1 %copy-start.65 = (f32[1,1,1024]{2,1,0:T(1,128)S(1)}, f32[1,1,1024]{2,1,0:T(1,128)}, u32[]{:S(2)}) copy-start(f32[1,1,1024]{2,1,0:T(1,128)} %get-tuple-element.482) | copy-start | bytes 12292
  77.5 69.1 %copy-start.95 = (f32[1,1,1024]{2,1,0:T(1,128)S(1)}, f32[1,1,1024]{2,1,0:T(1,128)}, u32[]{:S(2)}) copy-start(f32[1,1,1024]{2,1,0:T(1,128)} %get-tuple-element.486) | copy-start | bytes 12292
  77.5 150.8 %all-reduce.22.cloned.1.call-start = ((), (), s32[]{:S(2)}) async-start(), calls=%async_computation.6 | async-start | bytes 4194304 | tf_op jit(solution)/shard_map/psum | solution.py:168
  145.6 14.4 copy-start.58
  146.5 13.5 copy-start.87
  146.6 13.5 copy-start.74
  146.7 14.7 copy-start.108
  165.1 170.3 %all-reduce.24.cloned.1.call-start = ((), (), s32[]{:S(2)}) async-start(), calls=%async_computation.7 | async-start | bytes 4194304 | tf_op jit(solution)/shard_map/psum | solution.py:157
  231.3 7.5 copy-start.6
  231.4 7.5 copy-start.61
  232.0 6.9 copy-start.79
  268.1 70.7 %copy-start.50 = (bf16[2,4,128,4,128]{4,3,2,1,0:T(4,128)(2,1)}, bf16[2,4,128,4,128]{4,3,2,1,0:T(4,128)(2,1)S(1)}, u32[]{:S(2)}) copy-start(bf16[2,4,128,4,128]{4,3,2,1,0:T(4,128)(2,1)S(1)} %copy.158) | copy-start | bytes 3145732
  272.4 154.6 %all-reduce.26.cloned.1.call-start = ((), (), s32[]{:S(2)}) async-start(), calls=%async_computation.8 | async-start | bytes 4194304 | tf_op jit(solution)/shard_map/psum | solution.py:209
  338.8 16.0 %copy-start.10 = (f32[1024,1024]{1,0:T(8,128)}, f32[1024,1024]{1,0:T(8,128)S(1)}, u32[]{:S(2)}) copy-start(f32[1024,1024]{1,0:T(8,128)S(1)} %get-tuple-element.452) | copy-start | bytes 12582916
  338.9 93.0 %copy-start.70 = (f32[1024]{0:T(1024)}, f32[1024]{0:T(1024)S(1)}, u32[]{:S(2)}) copy-start(f32[1024]{0:T(1024)S(1)} %broadcast_multiply_fusion) | copy-start | bytes 12292
  339.4 92.4 %copy-start.77 = (f32[1024]{0:T(1024)}, f32[1024]{0:T(1024)S(1)}, u32[]{:S(2)}) copy-start(f32[1024]{0:T(1024)S(1)} %fusion.168) | copy-start | bytes 12292
  342.5 12.2 copy-start.35
  342.5 12.2 copy-start.109
  363.9 209.4 %all-reduce.28.cloned.1.call-start = ((), (), s32[]{:S(2)}) async-start(), calls=%async_computation.9 | async-start | bytes 4194304 | tf_op jit(solution)/shard_map/psum | solution.py:239
  505.6 67.7 %copy-start.62 = (f32[1024]{0:T(1024)S(1)}, f32[1024]{0:T(1024)}, u32[]{:S(2)}) copy-start(f32[1024]{0:T(1024)} %copy-done.61) | copy-start | bytes 12292
  505.6 67.7 %copy-start.69 = (f32[1,1,1024]{2,1,0:T(1,128)S(1)}, f32[1,1,1024]{2,1,0:T(1,128)}, u32[]{:S(2)}) copy-start(f32[1,1,1024]{2,1,0:T(1,128)} %get-tuple-element.484) | copy-start | bytes 12292
  510.2 67.3 %copy-start.90 = (f32[1024]{0:T(1024)S(1)}, f32[1024]{0:T(1024)}, u32[]{:S(2)}) copy-start(f32[1024]{0:T(1024)} %copy-done.89) | copy-start | bytes 12292
  510.2 67.4 %copy-start.80 = (f32[1024]{0:T(1024)S(1)}, f32[1024]{0:T(1024)}, u32[]{:S(2)}) copy-start(f32[1024]{0:T(1024)} %copy-done.79) | copy-start | bytes 12292
  510.3 148.3 %all-reduce.30.cloned.1.call-start = ((), (), s32[]{:S(2)}) async-start(), calls=%async_computation.10 | async-start | bytes 4194304 | tf_op jit(solution)/shard_map/psum | solution.py:209
  580.6 6.2 copy-start.117
  582.6 7.8 copy-start.29
  595.5 255.0 %all-reduce.34.cloned.1.call-start = ((), (), s32[]{:S(2)}) async-start(), calls=%async_computation.17 | async-start | bytes 8388608 | tf_op jit(solution)/shard_map/psum | solution.py:168
  595.5 63.0 %copy-start.1 = (bf16[1024,1024]{1,0:T(8,128)(2,1)S(1)}, bf16[1024,1024]{1,0:T(8,128)(2,1)}, u32[]{:S(2)}) copy-start(bf16[1024,1024]{1,0:T(8,128)(2,1)} %param.17) | copy-start | bytes 6291460
  595.5 63.0 %copy-start.59 = (f32[1024]{0:T(1024)S(1)}, f32[1024]{0:T(1024)}, u32[]{:S(2)}) copy-start(f32[1024]{0:T(1024)} %copy-done.58) | copy-start | bytes 12292
  595.5 63.0 %copy-start.66 = (f32[1,1,1024]{2,1,0:T(1,128)S(1)}, f32[1,1,1024]{2,1,0:T(1,128)}, u32[]{:S(2)}) copy-start(f32[1,1,1024]{2,1,0:T(1,128)} %get-tuple-element.482) | copy-start | bytes 12292
  601.6 60.9 %copy-start.88 = (f32[1024]{0:T(1024)S(1)}, f32[1024]{0:T(1024)}, u32[]{:S(2)}) copy-start(f32[1024]{0:T(1024)} %copy-done.87) | copy-start | bytes 12292
  601.6 60.9 %copy-start.75 = (f32[1024]{0:T(1024)S(1)}, f32[1024]{0:T(1024)}, u32[]{:S(2)}) copy-start(f32[1024]{0:T(1024)} %copy-done.74) | copy-start | bytes 12292
  672.4 6.2 copy-start.57
  742.1 10.4 copy-start.92
  742.1 10.4 copy-start.91
  742.1 10.4 copy-start.2
  742.1 10.4 copy-start.64
  742.1 10.4 copy-start.73
  742.1 10.4 copy-start.86
  742.2 10.4 copy-start.100
  742.2 193.7 %reduce-scatter.18.cloned.1.call-start = ((), (), s32[]{:S(2)}) async-start(), calls=%async_computation.15 | async-start | bytes 557056
  742.8 9.8 copy-start.53
  758.7 96.8 %copy-start.84 = (f32[1024]{0:T(1024)S(1)}, f32[1024]{0:T(1024)}, u32[]{:S(2)}) copy-start(f32[1024]{0:T(1024)} %copy-done.83) | copy-start | bytes 12292
  855.5 114.9 %reduce-scatter.16.cloned.1.call-start = ((), (), s32[]{:S(2)}) async-start(), calls=%async_computation.14 | async-start | bytes 557056
  861.5 344.6 %all-reduce.32.cloned.1.call-start = ((), (), s32[]{:S(2)}) async-start(), calls=%async_computation.16 | async-start | bytes 25165824
  893.1 390.3 %reduce-scatter.10.cloned.1.call-start = ((), (), s32[]{:S(2)}) async-start(), calls=%async_computation.11 | async-start | bytes 4456448 | tf_op jit(solution)/shard_map/reduce_scatter | solution.py:261
  900.5 491.1 %reduce-scatter.14.cloned.1.call-start = ((), (), s32[]{:S(2)}) async-start(), calls=%async_computation.13 | async-start | bytes 8912896 | tf_op jit(solution)/shard_map/reduce_scatter | solution.py:263
  912.1 6.4 copy-start.60
  912.1 6.4 copy-start.67
  912.1 6.4 copy-start.76
  912.1 6.4 copy-start.96
  912.1 588.5 %reduce-scatter.12.cloned.1.call-start = ((), (), s32[]{:S(2)}) async-start(), calls=%async_computation.12 | async-start | bytes 8912896 | tf_op jit(solution)/shard_map/reduce_scatter | solution.py:262
  912.7 5.7 copy-start.14
  912.8 5.7 copy-start.119
  927.5 5.2 copy-start.25
  927.5 5.2 copy-start.28
  (83 other events, 232.8 us)
Sparse Core Ops, SparseCore 0:
  77.6 65.5 all-reduce.19
  165.3 62.9 all-reduce.21
  272.5 62.8 all-reduce.23
  364.1 62.8 all-reduce.25
  510.4 62.9 all-reduce.27
  595.6 62.9 all-reduce.29
  742.2 108.2 all-reduce.33
  855.6 55.7 reduce-scatter.17
  915.5 54.8 reduce-scatter.15
  974.5 231.5 all-reduce.31
  1211.0 72.3 reduce-scatter.9
  1287.9 103.7 reduce-scatter.13
  1396.3 104.3 reduce-scatter.11
where the time goes:
time: 1520 us; the launch traced here: 1510 us
  waiting for transfers between devices  1020 us (67%)
  local copies, waits for them, and re-layouts  194 us (13%)
  matrix products  177 us (12%)
  other arithmetic  96.4 us (6%)
  between operations  16.3 us (1%)
    unnamed x16, waiting for transfers between devices  267 us
    psum x2, waiting for transfers between devices, local(): lax.psum(contract_last(active, w_down[layer]).astype(jnp.bfloat16), 'tens...  150 us
    psum x2, waiting for transfers between devices, local(): lax.psum(contract_last(mixed, w_out[layer]).astype(jnp.bfloat16), 'tensor')  128 us
    psum x2, waiting for transfers between devices, local(): lax.psum(contract_last(grad_upward, w_up[layer]).astype(jnp.bfloat16), 't...  120 us
    reduce_scatter x1, waiting for transfers between devices, local(): lax.psum_scatter(stacked[2], 'dp', scatter_dimension=1, tiled=True)  109 us
    reduce_scatter x1, waiting for transfers between devices, local(): lax.psum_scatter(stacked[3], 'dp', scatter_dimension=1, tiled=True)  108 us
    reduce_scatter x1, waiting for transfers between devices, local(): lax.psum_scatter(stacked[1], 'dp', scatter_dimension=1, tiled=True)  74.9 us
    psum x1, waiting for transfers between devices, local(): lax.psum(contract_last(grad_projected, w_qkv[layer].reshape(width, 3 * co...  62.9 us
  transfers between devices with their start and end apart: 13, of which 12 were waited for; matrix products, arithmetic and copies ran while one was open for 7% of the time, Pallas kernels for 0%

commit v1 on v0

v1 whole, which is shorter than its diff:
```python
import functools
from types import SimpleNamespace

import jax
import jax.numpy as jnp
from jax import lax
from jax.experimental import pallas as pl
from jax.experimental.pallas import tpu as pltpu
from jax.sharding import PartitionSpec as P

HEAD_DIM = 128
TILE = 64
EPS = 1e-05
MASKED = -1e30
MESH = pl.DeviceIdType.MESH
VMEM = pltpu.VMEM
ANY = pl.ANY
F32 = jnp.float32
BF16 = jnp.bfloat16
SCALE = HEAD_DIM**-0.5
VMEM_LIMIT = 62 << 20
GROUP = 16
CHUNK = 32

ERFC = (
    0.22567586600780487,
    0.22566960752010345,
    0.20784251391887665,
    0.16854380071163177,
    0.14142295718193054,
    -0.005586510524153709,
    0.1690569967031479,
    -0.18288171291351318,
    0.05025661736726761,
)


def dot_nn(a, b):
    return lax.dot_general(a, b, (((1,), (0,)), ((), ())), preferred_element_type=F32)


def dot_nt(a, b):
    return lax.dot_general(a, b, (((1,), (1,)), ((), ())), preferred_element_type=F32)


def dot_tn(a, b):
    return lax.dot_general(a, b, (((0,), (0,)), ((), ())), preferred_element_type=F32)


def rows_at(index, size):
    return pl.ds(pl.multiple_of(index * size, size), size)


def flip(value, bit):
    return value + bit * (1 - 2 * lax.rem(value // bit, 2))


def normalize(x):
    center = x - jnp.mean(x, axis=-1, keepdims=True)
    spread = lax.rsqrt(jnp.mean(center * center, axis=-1, keepdims=True) + EPS)
    return center * spread, spread


def gelu_parts(u):
    t = 1.0 / (1.0 + (0.4 * 0.7071067811865476) * jnp.abs(u))
    q = jnp.full_like(t, ERFC[-1])
    for c in ERFC[-2::-1]:
        q = q * t + c
    e = jnp.exp(-0.5 * (u * u))
    tail = 0.5 * (t * q) * e
    cdf = jnp.where(u >= 0, 1.0 - tail, tail)
    return u * cdf, cdf + u * (e * 0.3989422804014327)


class Copies:
    def __init__(self, sems):
        self.sems, self.n, self.open = sems, 0, []

    def start(self, src, dst):
        assert self.n < self.sems.shape[0]
        copy = pltpu.make_async_copy(src, dst, self.sems.at[self.n])
        self.n += 1
        copy.start()
        return copy

    def save(self, src, dst):
        self.open.append(self.start(src, dst))
        return self.open[-1]

    def settle(self, copy):
        self.open.remove(copy)
        copy.wait()

    def finish(self):
        for copy in self.open:
            copy.wait()


class Remote:
    def __init__(self, send, recv):
        self.send, self.recv, self.n, self.sent = send, recv, 0, []

    def start(self, src, dst, device):
        assert self.n < self.send.shape[0]
        copy = pltpu.make_async_remote_copy(
            src_ref=src,
            dst_ref=dst,
            send_sem=self.send.at[self.n],
            recv_sem=self.recv.at[self.n],
            device_id=device,
            device_id_type=MESH,
        )
        self.n += 1
        copy.start()
        self.sent.append(copy)
        return copy

    def finish(self):
        for copy in self.sent:
            copy.wait_send()


def greet(devices):
    barrier = pltpu.get_barrier_semaphore()
    for device in devices:
        pl.semaphore_signal(barrier, inc=1, device_id=device, device_id_type=MESH)
    pl.semaphore_wait(barrier, len(devices))


class Gather:
    def __init__(self, remote, own, other, order):
        self.remote, self.own, self.other, self.order = remote, own, other, order
        me, t = lax.axis_index("dp"), lax.axis_index("tensor")
        self.me, self.t = me, t
        self.have = [lax.rem(me, 8)]
        self.stage = 0
        self.flying = []

    def block(self, ref, index):
        size = ref.shape[0] // 8
        return ref.at[rows_at(index, size), :]

    def first(self):
        b = self.have[0]
        self.flying = [
            self.remote.start(
                self.block(self.own, b), self.block(self.other, b), (self.me, 1 - self.t)
            )
        ]

    def step(self):
        for copy in self.flying:
            copy.wait_recv()
        if self.stage == 3:
            return
        if self.stage > 0:
            bit = self.order[self.stage - 1]
            self.have = self.have + [flip(b, bit) for b in self.have]
        bit = self.order[self.stage]
        self.stage += 1
        device = (flip(self.me, bit), self.t)
        self.flying = [
            self.remote.start(self.block(self.other, b), self.block(self.other, b), device)
            for b in self.have
        ]


class Scatter:
    BITS = (1, 2, 4, 8)

    def __init__(self, remote, grad, recvs, stage=0):
        self.remote, self.grad, self.recvs, self.stage = remote, grad, recvs, stage
        self.me, self.t = lax.axis_index("dp"), lax.axis_index("tensor")
        self.base = 0
        self.count = 16 >> stage

    def send(self):
        bit = self.BITS[self.stage]
        mine = lax.rem(self.me // bit, 2)
        half = self.count // 2
        out = self.base + (1 - mine) * half
        self.base = self.base + mine * half
        self.count = half
        self.flying = self.remote.start(
            self.grad.at[pl.ds(out, half)],
            self.recvs[self.stage],
            (flip(self.me, bit), self.t),
        )

    def add(self):
        self.flying.wait_recv()
        recv = self.recvs[self.stage]
        self.stage += 1

        def body(i, carry):
            at = self.base + i
            self.grad[at] = (self.grad[at].astype(F32) + recv[i].astype(F32)).astype(BF16)
            return carry

        lax.fori_loop(0, self.count, body, 0)

    def step(self):
        self.add()
        self.send()

    def last(self):
        self.flying.wait_recv()
        return self.grad[self.base].astype(F32) + self.recvs[self.stage][0].astype(F32)


def forward_kernel(layer, names, *args):
    r = SimpleNamespace(**dict(zip(names, args)))
    copies = Copies(r.sem)
    remote = Remote(r.send, r.recv)
    me, t = lax.axis_index("dp"), lax.axis_index("tensor")
    rows, width = r.x.shape
    cols = r.qkv_own.shape[-1]
    heads = cols // HEAD_DIM
    half = r.up_own.shape[-1]
    pieces = width // cols

    x_load = copies.start(r.x_in, r.x_raw if layer == 0 else r.x)
    greet([(me, 1 - t), (flip(me, 2), t), (flip(me, 4), t), (flip(me, 1), t)])

    own = [r.qkv_own.at[layer, j] for j in range(3)]
    one, two = (2, 4, 1), (4, 2, 1)
    if layer == 0:
        other = [r.qkv_oth.at[j] for j in range(3)]
        gq = [Gather(remote, own[j], other[j], two if j == 1 else one) for j in range(3)]
        go = Gather(remote, r.out_own.at[0], r.out_oth, two)
        gu = Gather(remote, r.up_own.at[0], r.up_oth, one)
        gd = Gather(remote, r.dn_own.at[0], r.dn_oth, two)
        nq = [
            Gather(remote, r.qkv_own.at[1, j], r.qkv_nxt.at[j], one if j == 1 else two)
            for j in range(3)
        ]
        no = Gather(remote, r.out_own.at[1], r.out_nxt, one)
        for g in (*gq, go, gu, gd):
            g.first()
    else:
        gu = Gather(remote, r.up_own.at[1], r.up_oth, one)
        gd = Gather(remote, r.dn_own.at[1], r.dn_oth, two)
        gu.first()
        gd.first()

    w_load = [copies.start(own[j], r.wq.at[j]) for j in range(3)]
    bias_load = copies.start(r.bias, r.mask)
    wo_load = [copies.start(r.out_own.at[layer], r.wo.at[0]), None]
    wu_load = [copies.start(r.up_own.at[layer], r.wu.at[0]), None]
    wd_load = [copies.start(r.dn_own.at[layer], r.wd.at[0]), None]
    if layer == 1:
        w_load += [copies.start(r.qkv_oth.at[j], r.wq.at[3 + j]) for j in range(3)]
        wo_load[1] = copies.start(r.out_oth, r.wo.at[1])

    x = r.x

    def norm(which, h, xh, spread, source=None):
        gain = r.gain[which : which + 1, :]
        shift = r.shift[which : which + 1, :]

        def body(i, carry):
            at = rows_at(i, CHUNK)
            if source is not None:
                values = source[at, :].astype(F32)
                x[at, :] = values
            else:
                values = x[at, :]
            hat, rs = normalize(values)
            xh[at, :] = hat.astype(BF16)
            h[at, :] = (hat * gain + shift).astype(BF16)
            spread[at, :] = jnp.broadcast_to(rs, (CHUNK, HEAD_DIM))
            return carry

        lax.fori_loop(0, rows // CHUNK, body, 0)

    x_load.wait()
    norm(0, r.h1, r.xh1, r.r1, r.x_raw if layer == 0 else None)
    h1_save = copies.save(r.h1, r.h1_out)
    copies.save(r.xh1, r.xh1_out)
    copies.save(r.r1, r.r1_out)

    qkv, wq = r.qkv, r.wq

    def project(j):
        qkv[j] = dot_nn(r.h1[...], wq[j]).astype(BF16)

    def attend(group, start, stop):
        lane = lax.broadcasted_iota(jnp.int32, (TILE, HEAD_DIM), 1)

        def body(i, carry):
            q_at = rows_at(i, TILE)
            k_at = pl.ds(pl.multiple_of(jnp.maximum(i - 1, 0) * TILE, TILE), 2 * TILE)
            mask = r.mask[q_at, :]
            kept = jnp.zeros((TILE, HEAD_DIM), F32)
            for head in range(heads):
                c = slice(head * HEAD_DIM, (head + 1) * HEAD_DIM)
                s = dot_nt(qkv[3 * group, q_at, c], qkv[3 * group + 1, k_at, c]) * SCALE + mask
                top = jnp.max(s, axis=-1, keepdims=True)
                e = jnp.exp(s - top)
                total = jnp.sum(e, axis=-1, keepdims=True)
                p = (e * (1.0 / total)).astype(BF16)
                mixed = dot_nn(p, qkv[3 * group + 2, k_at, c])
                r.o[group, q_at, c] = mixed.astype(BF16)
                kept = jnp.where(lane == head, top + jnp.log(total), kept)
            r.lse[group, q_at, :] = kept
            return carry

        lax.fori_loop(start, stop, body, 0)

    def out_project(group):
        def body(n, carry):
            at = rows_at(n, cols)
            x[:, at] += dot_nt(r.o[group], r.wo[group, at, :])
            return carry

        lax.fori_loop(0, pieces, body, 0)

    tiles = rows // TILE
    quarter = tiles // 4
    for j in range(3):
        w_load[j].wait()
        project(j)
        if layer == 0:
            if j == 0:
                gq[0].step()
            if j == 2:
                gq[1].step()
    bias_load.wait()
    for i in range(4):
        attend(0, i * quarter, (i + 1) * quarter)
        if layer == 0:
            (lambda: gq[0].step(), lambda: gq[2].step(), lambda: gq[1].step(), lambda: go.step())[i]()
    copies.save(r.o.at[0], r.o_out)
    wo_load[0].wait()
    out_project(0)

    if layer == 0:
        gq[2].step()
        gq[0].step()
        gu.step()
        gq[1].step()
        gq[0].step()
        w_load.append(copies.start(other[0], wq.at[3]))
        go.step()
        gq[2].step()
        for g in nq:
            g.first()
        no.first()
    w_load[3].wait()
    project(3)
    if layer == 0:
        gq[1].step()
        w_load.append(copies.start(other[1], wq.at[4]))
        gu.step()
        gd.step()
    w_load[4].wait()
    project(4)
    if layer == 0:
        gq[2].step()
        w_load.append(copies.start(other[2], wq.at[5]))
        go.step()
    w_load[5].wait()
    project(5)
    if layer == 1:
        gu.step()
        gd.step()
    copies.save(qkv, r.qkv_out)
    for i in range(4):
        attend(1, i * quarter, (i + 1) * quarter)
        if layer == 0:
            if i == 0:
                go.step()
                wo_load[1] = copies.start(r.out_oth, r.wo.at[1])
                gu.step()
            if i == 1:
                gd.step()
            if i == 2:
                gu.step()
                wu_load[1] = copies.start(r.up_oth, r.wu.at[1])
                nq[0].step()
            if i == 3:
                gd.step()
        else:
            if i == 0:
                gu.step()
            if i == 1:
                gd.step()
            if i == 2:
                gu.step()
            if i == 3:
                gd.step()
    copies.save(r.lse, r.lse_out)
    wo_load[1].wait()
    out_project(1)
    if layer == 0:
        gd.step()
        wd_load[1] = copies.start(r.dn_oth, r.wd.at[1])
        nq[1].step()
    else:
        gu.step()
        wu_load[1] = copies.start(r.up_oth, r.wu.at[1])
        gd.step()
        wd_load[1] = copies.start(r.dn_oth, r.wd.at[1])

    norm(1, r.h2, r.xh2, r.r2)
    copies.save(r.h2, r.h2_out)
    copies.save(r.xh2, r.xh2_out)
    copies.save(r.r2, r.r2_out)
    if layer == 0:
        nq[2].step()
        nq[0].step()

    def up(group):
        def body(n, carry):
            at = rows_at(n, cols)
            r.u[...] = dot_nn(r.h2[...], r.wu[group, :, at])

            def inner(i, carry):
                i_at = rows_at(i, CHUNK)
                a, d = gelu_parts(r.u[i_at, :])
                r.a[group, i_at, at] = a.astype(BF16)
                r.d[group, i_at, at] = d.astype(BF16)
                return carry

            return lax.fori_loop(0, rows // CHUNK, inner, carry)

        lax.fori_loop(0, half // cols, body, 0)
        if group == 0:
            copies.save(r.a.at[0], r.a_out)
        copies.save(r.d.at[group], r.d_out.at[group])

    def down(group):
        def body(n, carry):
            at = rows_at(n, cols)
            x[:, at] += dot_nt(r.a[group], r.wd[group, at, :])
            return carry

        lax.fori_loop(0, pieces, body, 0)

    wu_load[0].wait()
    up(0)
    if layer == 0:
        no.step()
        nq[1].step()
        nq[0].step()
    wu_load[1].wait()
    up(1)
    if layer == 0:
        nq[2].step()
        no.step()
        nq[1].step()
        nq[0].step()
    wd_load[0].wait()
    down(0)
    if layer == 0:
        nq[2].step()
        no.step()
        nq[1].step()
    wd_load[1].wait()
    down(1)
    if layer == 0:
        copies.save(x, r.y_out)
        nq[2].step()
        no.step()
    else:
        copies.settle(h1_save)

        def body(i, carry):
            at = rows_at(i, CHUNK)
            r.h1[at, :] = x[at, :].astype(BF16)
            return carry

        lax.fori_loop(0, rows // CHUNK, body, 0)
        copies.save(r.h1, r.y_out)
    copies.finish()
    remote.finish()


def backward_kernel(layer, reduce, names, *args):
    r = SimpleNamespace(**dict(zip(names, args)))
    copies = Copies(r.sem)
    me, t = lax.axis_index("dp"), lax.axis_index("tensor")
    L, g, dh = r.L, r.g, r.dh
    rows, width = g.shape
    cols = r.qkv_own.shape[-1]
    heads = cols // HEAD_DIM
    half = r.up_own.shape[-1]
    pieces = width // cols

    if reduce:
        remote = Remote(r.send, r.recv)
        if layer == 1:
            greet([(flip(me, b), t) for b in (1, 2, 4, 8)])
        else:
            low = lax.rem(me, GROUP)
            greet([(me - low + lax.rem(low + o, GROUP), t) for o in range(1, GROUP)])
        s_dn = Scatter(remote, r.dn_g, [r.dn_r0, r.dn_r1, r.dn_r2, r.dn_r3])
        s_up = Scatter(remote, r.up_g, [r.up_r0, r.up_r1, r.up_r2, r.up_r3])
        s_out = Scatter(remote, r.out_g, [r.out_r0, r.out_r1, r.out_r2, r.out_r3])
        if layer == 0:
            s_qkv = Scatter(remote, r.qkv_g, [r.qkv_r0, r.qkv_r1, r.qkv_r2, r.qkv_r3])
            s_old = Scatter(remote, r.old_g, [None, r.old_r1, r.old_r2, r.old_r3], 1)
        else:
            s_qkv = Scatter(remote, r.qkv_g, [r.qkv_r0])

    g_load = copies.start(r.g_in, L.at[0] if layer == 1 else g)
    if reduce and layer == 0:
        old_load = copies.start(r.old_in, r.old_g)
    halves = [slice(i * cols, (i + 1) * cols) for i in range(pieces)]
    wd_load = [
        copies.start(r.dn_own.at[layer], L.at[3]),
        copies.start(r.dn_oth, L.at[4]),
    ]
    d_load = [copies.start(r.d.at[i], L.at[5 + i]) for i in range(2)]
    a_load = copies.start(r.a, L.at[7])
    h2_load = copies.start(r.h2, L.at[8])
    wu_load = [
        copies.start(r.up_own.at[layer], L.at[9]),
        copies.start(r.up_oth, L.at[10]),
    ]
    xh_load = copies.start(r.xh2, L.at[11])
    r2_load = copies.start(r.r2, r.spread)
    wo_load = [
        copies.start(r.out_own.at[layer], L.at[12, :, halves[0]]),
        copies.start(r.out_oth, L.at[12, :, halves[1]]),
    ]
    o_load = copies.start(r.o, L.at[13, :, halves[0]])
    mask_load = copies.start(r.bias, r.mask)
    lse_load = copies.start(r.lse, r.lse_v)

    def zero(i, carry):
        r.sums[i] = jnp.zeros((8, width), F32)
        return carry

    lax.fori_loop(0, 4, zero, 0)

    g_load.wait()

    def begin(i, carry):
        at = rows_at(i, CHUNK)
        if layer == 1:
            g[at, :] = L[0, at, :].astype(F32)
        else:
            L[0, at, :] = g[at, :].astype(BF16)
        return carry

    lax.fori_loop(0, rows // CHUNK, begin, 0)
    if reduce and layer == 0:
        old_load.wait()
        s_old.send()

    def du(group):
        def body(n, carry):
            at = rows_at(n, cols)
            da = dot_nn(L[0], L[3 + group, :, at])
            L[1 + group, :, at] = (da * L[5 + group, :, at].astype(F32)).astype(BF16)
            return carry

        lax.fori_loop(0, half // cols, body, 0)

    def weight_grad(lhs, rhs, out, at):
        full = dot_tn(lhs, rhs)
        size = width // GROUP
        for d in range(GROUP):
            pos = (d % 2) * 8 + (d // 2 % 2) * 4 + (d // 4 % 2) * 2 + d // 8
            out[pos, :, at] = full[d * size : (d + 1) * size].astype(BF16)

    for i in range(2):
        wd_load[i].wait()
        d_load[i].wait()
        du(i)
    qkv_load = [
        copies.start(r.qkv.at[j], L.at[3 + j // 2, :, halves[j % 2]]) for j in range(6)
    ]

    a_load.wait()

    def down_grad(n, carry):
        at = rows_at(n, cols)
        weight_grad(L[0], L[7, :, at], r.dn_g, at)
        return carry

    lax.fori_loop(0, half // cols, down_grad, 0)
    if reduce:
        s_dn.send()
    h2_load.wait()

    def up_grad(n, carry):
        at = rows_at(n, cols)
        weight_grad(L[8], L[1, :, at], r.up_g, at)
        return carry

    lax.fori_loop(0, half // cols, up_grad, 0)
    h1_load = copies.start(r.h1, L.at[8])
    if reduce:
        if layer == 0:
            s_old.step()
        s_dn.step()
        s_up.send()

    for i in range(2):
        wu_load[i].wait()

    def dh2(n, carry):
        at = rows_at(n, cols)
        dh[:, at] = dot_nt(L[1], L[9, at, :]) + dot_nt(L[2], L[10, at, :])
        return carry

    lax.fori_loop(0, pieces, dh2, 0)
    wq_load = [
        copies.start(
            r.qkv_own.at[layer, j] if j < 3 else r.qkv_oth.at[j - 3],
            L.at[9 + j // 2, :, halves[j % 2]],
        )
        for j in range(4)
    ]
    if reduce:
        s_up.step()

    def norm_back(which, spread):
        gain = r.gain[which : which + 1, :]

        def body(i, carry):
            at = rows_at(i, CHUNK)
            hat = L[11, at, :].astype(F32)
            grad = dh[at, :]
            rs = spread[at, 0:1]
            e = grad * gain
            prod = grad * hat
            m1 = jnp.mean(e, axis=-1, keepdims=True)
            m2 = jnp.mean(e * hat, axis=-1, keepdims=True)
            new = g[at, :] + rs * (e - m1 - hat * m2)
            g[at, :] = new
            L[0, at, :] = new.astype(BF16)
            r.sums[which] += jnp.sum(prod.reshape(CHUNK // 8, 8, width), axis=0)
            r.sums[2 + which] += jnp.sum(grad.reshape(CHUNK // 8, 8, width), axis=0)
            return carry

        lax.fori_loop(0, rows // CHUNK, body, 0)

    xh_load.wait()
    r2_load.wait()
    norm_back(1, r.spread)
    xh1_load = copies.start(r.xh1, L.at[11])
    r1_load = copies.start(r.r1, r.spread)

    for i in range(2):
        wo_load[i].wait()
        L[6, :, halves[i]] = dot_nn(L[0], L[12, :, halves[i]]).astype(BF16)
    wq_load += [
        copies.start(r.qkv_oth.at[j - 3], L.at[12, :, halves[j % 2]]) for j in range(4, 6)
    ]
    if reduce:
        if layer == 0:
            s_old.step()
        s_dn.step()
    o_load.wait()
    weight_grad(L[0], L[13, :, halves[0]], r.out_g, slice(0, cols))
    if reduce:
        s_out.send()

    place = [(3, 0), (3, 1), (4, 0), (4, 1), (5, 0), (5, 1)]
    to = [(1, 0), (1, 1), (2, 0), (2, 1), (7, 0), (7, 1)]

    def clear(i, carry):
        dh[rows_at(i, CHUNK), :] = jnp.zeros((CHUNK, width), F32)
        return carry

    def attend(group, start, stop):
        def part(j, at, head):
            slot, side = place[3 * group + j]
            begin_at = side * cols + head * HEAD_DIM
            return L[slot, at, begin_at : begin_at + HEAD_DIM]

        def body(i, carry):
            q_at = rows_at(i, TILE)
            k_at = pl.ds(pl.multiple_of(jnp.maximum(i - 1, 0) * TILE, TILE), 2 * TILE)
            mask = r.mask[q_at, :]
            kept = r.lse_v[group, q_at, :]
            for head in range(heads):
                q, k, v = part(0, q_at, head), part(1, k_at, head), part(2, k_at, head)
                at = group * cols + head * HEAD_DIM
                do = L[6, q_at, at : at + HEAD_DIM]
                s = dot_nt(q, k) * SCALE + mask
                p = jnp.exp(s - kept[:, head : head + 1])
                dp = dot_nt(do, v)
                inner = jnp.sum(dp * p, axis=-1, keepdims=True)
                ds = (p * (dp - inner)).astype(BF16)
                dq = dot_nn(ds, k) * SCALE
                slot, side = to[3 * group]
                at = side * cols + head * HEAD_DIM
                L[slot, q_at, at : at + HEAD_DIM] = dq.astype(BF16)
                at = head * HEAD_DIM
                dh[k_at, at : at + HEAD_DIM] += dot_tn(ds, q)
                at = cols + head * HEAD_DIM
                dh[k_at, at : at + HEAD_DIM] += dot_tn(p.astype(BF16), do)
            return carry

        lax.fori_loop(start, stop, body, 0)

    def settle(group):
        def body(i, carry):
            at = rows_at(i, CHUNK)
            slot, side = to[3 * group + 1]
            L[slot, at, halves[side]] = (dh[at, halves[0]] * SCALE).astype(BF16)
            slot, side = to[3 * group + 2]
            L[slot, at, halves[side]] = dh[at, halves[1]].astype(BF16)
            return carry

        lax.fori_loop(0, rows // CHUNK, body, 0)

    for load in (*qkv_load, mask_load, lse_load):
        load.wait()
    tiles = rows // TILE
    mid = tiles // 2
    lax.fori_loop(0, rows // CHUNK, clear, 0)
    attend(0, 0, mid)
    if reduce:
        s_up.step()
        s_out.step()
    attend(0, mid, tiles)
    settle(0)
    h1_load.wait()
    for j in range(3):
        slot, side = to[j]
        weight_grad(L[8], L[slot, :, halves[side]], r.qkv_g, slice(j * cols, (j + 1) * cols))
    if reduce:
        s_qkv.send()
        s_dn.step()
        if layer == 0:
            finish_old = s_old.last()
            for j in range(3):
                r.old_f[j] = finish_old[:, j * cols : (j + 1) * cols]
            copies.save(r.old_f, r.old_out)

    lax.fori_loop(0, rows // CHUNK, clear, 0)
    attend(1, 0, mid)
    if reduce:
        s_out.step()
        if layer == 0:
            s_qkv.step()
        else:
            s_qkv.add()
            copies.save(r.qkv_g.at[pl.ds(s_qkv.base, 8)], r.qkv_out)
        s_up.step()
        r.dn_f[...] = s_dn.last()
        copies.save(r.dn_f, r.dn_out)
    attend(1, mid, tiles)
    settle(1)
    if reduce:
        s_out.step()
    for load in wq_load:
        load.wait()

    def dh1(n, carry):
        at = rows_at(n, cols)
        dh[:, at] = (
            dot_nt(L[1], L[9, at, :]) + dot_nt(L[2], L[10, at, :]) + dot_nt(L[7], L[12, at, :])
        )
        return carry

    lax.fori_loop(0, pieces, dh1, 0)
    if reduce:
        if layer == 0:
            s_qkv.step()
        r.up_f[...] = s_up.last()
        copies.save(r.up_f, r.up_out)
    xh1_load.wait()
    r1_load.wait()
    norm_back(0, r.spread)
    copies.save(g, r.g_out)
    for k in range(4):
        r.flat[k : k + 1, :] = jnp.sum(r.sums[k], axis=0, keepdims=True)
    if not reduce:
        copies.save(r.dn_g, r.dn_out)
        copies.save(r.up_g, r.up_out)
        copies.save(r.out_g, r.out_out)
        copies.save(r.qkv_g, r.qkv_out)
        copies.save(r.flat, r.flat_out)
        copies.finish()
        return
    r.out_f[...] = s_out.last()
    copies.save(r.out_f, r.out_out)
    if layer == 1:
        copies.save(r.flat, r.flat_out)
    else:
        r.both[0:4, :] = r.flat[...]
        r.both[4:8, :] = r.flat_in[...]
        sends = []
        for o in range(1, GROUP):
            to_dev = lax.rem(low + o, GROUP)
            sends.append(
                remote.start(
                    r.both.at[:, rows_at(to_dev // 2, 128)],
                    r.slots.at[o],
                    (me - low + to_dev, t),
                )
            )
        s_qkv.step()
        total = r.both[:, rows_at(low // 2, 128)]
        for o, copy in enumerate(sends):
            copy.wait_recv()
            total = total + r.slots[o + 1]
        r.flat_f[...] = total
        copies.save(r.flat_f, r.flat_out)
        done = s_qkv.last()
        for j in range(3):
            r.qkv_f[j] = done[:, j * cols : (j + 1) * cols]
        copies.save(r.qkv_f, r.qkv_out)
    copies.finish()
    remote.finish()


def call(kernel, ins, outs, scratch, name, collective, flops):
    split = lambda v: v if isinstance(v, tuple) else (v, ANY)
    in_items = {k: split(v) for k, v in ins.items()}
    out_items = {k: split(v) for k, v in outs.items()}
    names = (*in_items, *out_items, *scratch)
    params = dict(vmem_limit_bytes=VMEM_LIMIT, has_side_effects=True)
    if collective is not None:
        params.update(collective_id=collective)
    made = pl.pallas_call(
        functools.partial(kernel, names),
        out_shape=tuple(v for v, _ in out_items.values()),
        in_specs=[pl.BlockSpec(memory_space=s) for _, s in in_items.values()],
        out_specs=tuple(pl.BlockSpec(memory_space=s) for _, s in out_items.values()),
        scratch_shapes=list(scratch.values()),
        compiler_params=pltpu.CompilerParams(**params),
        cost_estimate=pl.CostEstimate(flops=flops, bytes_accessed=60 << 20, transcendentals=0),
        name=name,
    )(*(v for v, _ in in_items.values()))
    return SimpleNamespace(**dict(zip(out_items, made)))


def forward(layer, x, bias, gain, shift, weights, other):
    rows, width = x.shape
    w_qkv, w_out, w_up, w_dn = weights
    cols, half = w_qkv.shape[-1], w_up.shape[-1]
    shape = jax.ShapeDtypeStruct
    wide, slab = (rows, width), (rows, cols)
    ins = dict(
        x_in=x, bias=bias, gain=(gain, VMEM), shift=(shift, VMEM),
        qkv_own=w_qkv, out_own=w_out, up_own=w_up, dn_own=w_dn,
    )
    outs = {}
    qkv_s, out_s = shape(w_qkv.shape[1:], BF16), shape(w_out.shape[1:], BF16)
    up_s, dn_s = shape(w_up.shape[1:], BF16), shape(w_dn.shape[1:], BF16)
    if layer == 0:
        outs.update(qkv_oth=qkv_s, out_oth=out_s, qkv_nxt=qkv_s, out_nxt=out_s)
    else:
        ins.update(qkv_oth=other.qkv_nxt, out_oth=other.out_nxt)
    outs.update(
        up_oth=up_s, dn_oth=dn_s,
        h1_out=shape(wide, BF16), xh1_out=shape(wide, BF16), r1_out=shape((rows, 128), F32),
        qkv_out=shape((6, *slab), BF16), lse_out=shape((2, rows, 128), F32), o_out=shape(slab, BF16),
        h2_out=shape(wide, BF16), xh2_out=shape(wide, BF16), r2_out=shape((rows, 128), F32),
        a_out=shape((rows, half), BF16), d_out=shape((2, rows, half), BF16),
        y_out=shape(wide, F32 if layer == 0 else BF16),
    )
    copies = 128 if layer == 0 else 16
    scratch = dict(
        x=VMEM(wide, F32), h1=VMEM(wide, BF16), xh1=VMEM(wide, BF16), r1=VMEM((rows, 128), F32),
        h2=VMEM(wide, BF16), xh2=VMEM(wide, BF16), r2=VMEM((rows, 128), F32),
        qkv=VMEM((6, *slab), BF16), o=VMEM((2, *slab), BF16), lse=VMEM((2, rows, 128), F32),
        mask=VMEM((rows, 128), F32), u=VMEM(slab, F32),
        a=VMEM((2, rows, half), BF16), d=VMEM((2, rows, half), BF16),
        wq=VMEM((6, width, cols), BF16), wo=VMEM((2, width, cols), BF16),
        wu=VMEM((2, width, half), BF16), wd=VMEM((2, width, half), BF16),
        sem=pltpu.SemaphoreType.DMA((40,)),
        send=pltpu.SemaphoreType.DMA((copies,)), recv=pltpu.SemaphoreType.DMA((copies,)),
    )
    if layer == 0:
        scratch.update(x_raw=VMEM(wide, BF16))
    flops = 2 * rows * (6 * cols * width + 2 * cols * width + 4 * half * width)
    return call(
        functools.partial(forward_kernel, layer), ins, outs, scratch, "forward", layer, flops
    )


def backward(layer, reduce, g, bias, gain, weights, other, kept, before):
    rows, width = g.shape
    w_qkv, w_out, w_up, w_dn = weights
    cols, half = w_qkv.shape[-1], w_up.shape[-1]
    shape = jax.ShapeDtypeStruct
    wide = (rows, width)
    block = width // GROUP
    ins = dict(
        g_in=g, bias=bias, gain=(gain, VMEM),
        qkv_own=w_qkv, out_own=w_out, up_own=w_up, dn_own=w_dn,
        qkv_oth=other.qkv, out_oth=other.out, up_oth=other.up, dn_oth=other.dn,
    )
    ins.update(
        h1=kept.h1_out, xh1=kept.xh1_out, r1=kept.r1_out, qkv=kept.qkv_out, lse=kept.lse_out, o=kept.o_out,
        h2=kept.h2_out, xh2=kept.xh2_out, r2=kept.r2_out, a=kept.a_out, d=kept.d_out,
    )
    outs = dict(g_out=shape(wide, F32))
    grad = lambda n: VMEM((GROUP, block, n), BF16)
    recv = lambda k, n: VMEM((GROUP >> (k + 1), block, n), BF16)
    done = lambda n: VMEM((block, n), F32)
    all3 = 3 * cols
    scratch = dict(
        L=VMEM((14, *wide), BF16), g=VMEM(wide, F32), dh=VMEM(wide, F32),
        mask=VMEM((rows, 128), F32), lse_v=VMEM((2, rows, 128), F32), spread=VMEM((rows, 128), F32),
        sums=VMEM((4, 8, width), F32), flat=VMEM((4, width), F32),
        sem=pltpu.SemaphoreType.DMA((56,)),
        dn_g=grad(half), up_g=grad(half), out_g=grad(cols), qkv_g=grad(all3),
    )
    if not reduce:
        full = lambda n: shape((GROUP, block, n), BF16)
        outs.update(dn_out=full(half), up_out=full(half), out_out=full(cols), qkv_out=full(all3))
        outs.update(flat_out=shape((4, width), F32))
    else:
        copies = 4 * 4 + 3 + GROUP
        part = lambda n: shape((block, n), F32)
        outs.update(dn_out=part(half), up_out=part(half), out_out=part(cols))
        scratch.update(
            send=pltpu.SemaphoreType.DMA((copies,)), recv=pltpu.SemaphoreType.DMA((copies,)),
            dn_f=done(half), up_f=done(half), out_f=done(cols), qkv_r0=recv(0, all3),
            dn_r0=recv(0, half), dn_r1=recv(1, half), dn_r2=recv(2, half), dn_r3=recv(3, half),
            up_r0=recv(0, half), up_r1=recv(1, half), up_r2=recv(2, half), up_r3=recv(3, half),
            out_r0=recv(0, cols), out_r1=recv(1, cols), out_r2=recv(2, cols), out_r3=recv(3, cols),
        )
        if layer == 1:
            outs.update(flat_out=shape((4, width), F32), qkv_out=shape((8, block, all3), BF16))
        else:
            three = shape((3, block, cols), F32)
            outs.update(flat_out=shape((8, 128), F32), qkv_out=three, old_out=three)
            ins.update(old_in=before.qkv_out, flat_in=(before.flat_out, VMEM))
            scratch.update(
                qkv_r1=recv(1, all3), qkv_r2=recv(2, all3), qkv_r3=recv(3, all3),
                old_g=VMEM((8, block, all3), BF16),
                old_r1=recv(1, all3), old_r2=recv(2, all3), old_r3=recv(3, all3),
                old_f=VMEM((3, block, cols), F32), qkv_f=VMEM((3, block, cols), F32),
                both=VMEM((8, width), F32), slots=VMEM((GROUP, 8, 128), F32), flat_f=VMEM((8, 128), F32),
            )
    flops = 2 * rows * (2 * 6 * cols * width + 3 * cols * width + 6 * half * width)
    return call(
        functools.partial(backward_kernel, layer, reduce), ins, outs, scratch,
        "backward", 2 + layer if reduce else None, flops,
    )


def local(n_dp, tokens, lengths, w_qkv, w_out, w_up, w_down, norm_gain, norm_bias, cotangent):
    rows, width = tokens.shape
    cols = w_qkv.shape[3]
    items = lengths.shape[1]
    order = jnp.arange(items, dtype=jnp.int32)
    ends = jnp.sum(jnp.where(order[:, None] >= order[None, :], lengths, 0), axis=1)
    place = jnp.arange(rows, dtype=jnp.int32)
    start = jnp.max(jnp.where(ends[None, :] <= place[:, None], ends[None, :], 0), axis=1)
    window = jnp.maximum(place // TILE - 1, 0) * TILE
    key = window[:, None] + jnp.arange(2 * TILE, dtype=jnp.int32)[None, :]
    allowed = (key >= start[:, None]) & (key <= place[:, None])
    bias = jnp.where(allowed, 0.0, MASKED).astype(F32)

    weights = (jnp.transpose(w_qkv, (0, 2, 1, 3)), w_out, w_up, w_down)
    f0 = forward(0, tokens, bias, norm_gain[0], norm_bias[0], weights, None)
    f1 = forward(1, f0.y_out, bias, norm_gain[1], norm_bias[1], weights, f0)
    output = f1.y_out
    reduce = n_dp == GROUP
    oth0 = SimpleNamespace(qkv=f0.qkv_oth, out=f0.out_oth, up=f0.up_oth, dn=f0.dn_oth)
    oth1 = SimpleNamespace(qkv=f0.qkv_nxt, out=f0.out_nxt, up=f1.up_oth, dn=f1.dn_oth)
    b1 = backward(1, reduce, cotangent, bias, norm_gain[1], weights, oth1, f1, None)
    b0 = backward(0, reduce, b1.g_out, bias, norm_gain[0], weights, oth0, f0, b1)
    grad = b0.g_out
    out, up, dn = (
        jnp.stack(v)
        for v in ((b0.out_out, b1.out_out), (b0.up_out, b1.up_out), (b0.dn_out, b1.dn_out))
    )
    if reduce:
        qkv = jnp.transpose(jnp.stack([b0.qkv_out, b0.old_out]), (0, 2, 1, 3))
        side = lax.rem(lax.axis_index("dp"), 2)
        block = width // GROUP
        flat = b0.flat_out.reshape(2, 4, 128)
        flat = lax.dynamic_slice_in_dim(flat, side * block, block, axis=2)
    else:

        def total(both):
            n = both.shape[-1]
            both = both.astype(F32).reshape(2, 2, 2, 2, 2, width // GROUP, n)
            both = jnp.transpose(both, (0, 4, 3, 2, 1, 5, 6)).reshape(2, width, n)
            return lax.psum_scatter(both, "dp", scatter_dimension=1, tiled=True)

        out, up, dn = total(out), total(up), total(dn)
        qkv = total(jnp.stack([b0.qkv_out, b1.qkv_out]))
        qkv = qkv.reshape(*qkv.shape[:2], 3, cols)
        flat = jnp.stack([b0.flat_out, b1.flat_out])
        flat = lax.psum_scatter(flat, "dp", scatter_dimension=2, tiled=True)
    gain, shift = flat[:, :2], flat[:, 2:]
    return (output, grad, qkv, out, up, dn, gain, shift)


def solution(mesh):
    placed = (
        P("dp", None),
        P("dp", None),
        P(None, None, None, "tensor"),
        P(None, None, "tensor"),
        P(None, None, "tensor"),
        P(None, None, "tensor"),
        P(),
        P(),
        P("dp", None),
    )
    return jax.shard_map(
        functools.partial(local, mesh.shape["dp"]),
        mesh=mesh,
        in_specs=placed,
        out_specs=(
            P("dp", None),
            P("dp", None),
            P(None, "dp", None, "tensor"),
            P(None, "dp", "tensor"),
            P(None, "dp", "tensor"),
            P(None, "dp", "tensor"),
            P(None, None, "dp"),
            P(None, None, "dp"),
        ),
        check_vma=False,
    )
```

time: 1520 us -> 467 us (0.31)
  waiting for transfers between devices: 1020 us -> 0 us
  Pallas kernels: 0 us -> 442 us
  local copies, waits for them, and re-layouts: 194 us -> 7 us
  matrix products: 177 us -> 0 us
  other arithmetic: 96.4 us -> 7.54 us
    psum x7 -> x0, waiting for transfers between devices: 461 us -> none  [the longest x2 150 us: local(): lax.psum(contract_last(active, w_down[layer]).astype(jnp.bfloat16), 'tens...]
    pallas_call x0 -> x4, Pallas kernels: none -> 442 us  [call(): pl.pallas_call(functools.partial(kernel, names), out_shape=tuple((v for v...]
    reduce_scatter x3 -> x0, waiting for transfers between devices: 292 us -> none  [the longest x1 109 us: local(): lax.psum_scatter(stacked[2], 'dp', scatter_dimension=1, tiled=True)]
    unnamed x16 -> x0, waiting for transfers between devices: 267 us -> none
    dot_general x52 -> x0, matrix products: 177 us -> none  [the longest x8 36.4 us: contract_first(): lax.dot_general(left, right, (((0,), (0,)), ((), ())), preferred_element_...]
    unnamed x235 -> x18, local copies, waits for them, and re-layouts: 52.5 us -> 4.99 us
    reduce_sum x21 -> x1, other arithmetic: 46.2 us -> 0.76 us  [local(): jnp.sum(jnp.where(order[:, None] >= order[None, :], lengths, 0), axis=1)]
    another operation x18 -> x0, local copies, waits for them, and re-layouts: 43.3 us -> none  [the longest x1 19.4 us: local(): jnp.stack([layer_parts[index][member] for index in range(layers)])]
  transfers between devices with their start and end apart: 13 -> 0, of which waited for: 12 -> 0; matrix products, arithmetic and copies ran while one was open for 7% -> 0% of each run, Pallas kernels for 0% -> 0%
where the time goes in v1:
time: 467 us; the launch traced here: 458 us
  Pallas kernels  442 us (95%)
  other arithmetic  7.54 us (2%)
  local copies, waits for them, and re-layouts  7 us (1%)
    pallas_call x4, Pallas kernels, call(): pl.pallas_call(functools.partial(kernel, names), out_shape=tuple((v for v...  442 us

profile of v1, /device:TPU:0, one launch (start us, length us, event | category | flops | bytes accessed | tf_op | source)
XLA Modules:
  0.0 457.8 jit_solution(636642822108342079)
XLA Ops:
  0.6 0.8 select_reduce_fusion.1
  1.4 0.1 select_reduce_fusion
  1.5 1.1 fusion.2.args_1_
  2.7 1.4 slice_bitcast_fusion
  4.0 119.3 %forward.2 = (bf16[3,1024,512]{2,1,0:T(8,128)(2,1)}, bf16[1024,512]{1,0:T(8,128)(2,1)}, bf16[3,1024,512]{2,1,0:T(8,128)(2,1)}, bf16[1024,512]{1,0:T(8,128)(2,1)}...) custom-call(bf16[1024,1024]{1,0:T(8,128)(2,1)} %args_0_.5, ...), custom_call_target="tpu_custom_call" | custom-call | flops 17179869184 | bytes 62914560 | tf_op jit(solution)/shard_map/forward/pallas_call | solution.py:822
  123.3 98.0 %forward.3 = (bf16[1024,1024]{1,0:T(8,128)(2,1)}, bf16[1024,1024]{1,0:T(8,128)(2,1)}, bf16[1024,1024]{1,0:T(8,128)(2,1)}, bf16[1024,1024]{1,0:T(8,128)(2,1)}, f3...) custom-call(f32[1024,1024]{1,0:T(8,128)} %get-tuple-element.53.args_, ...), custom_call_target="tpu_custom_call" | custom-call | flops 17179869184 | bytes 62914560 | tf_op jit(solution)/shard_map/forward/pallas_call | solution.py:822
  221.3 103.2 %backward.2 = (f32[1024,1024]{1,0:T(8,128)}, f32[64,1024]{1,0:T(8,128)}, f32[64,1024]{1,0:T(8,128)}, f32[64,512]{1,0:T(8,128)}, f32[4,1024]{1,0:T(4,128)}, /*index=5*/bf16[8,64,1536]{2,1,0:T(8,128)(2,1)}) custom-call(bf16[1024,1024]{1,0:T(8,128)(2,1)} %args_0_.6, f32[1024,128]{1,0:T(8,128)} %fusion.2.args_1_, f32[2,1024]{1,0:T(2,128)} %get-tuple-element.105.args_2_, ...), custom_call_target="tpu_custom_call" | custom-call | flops 28991029248 | bytes 62914560 | tf_op jit(solution)/shard_map/backward/pallas_call | solution.py:822
  324.5 0.0 copy-start.6
  324.5 121.6 %backward.3 = (f32[1024,1024]{1,0:T(8,128)}, f32[64,1024]{1,0:T(8,128)}, f32[64,1024]{1,0:T(8,128)}, f32[64,512]{1,0:T(8,128)}, f32[8,128]{1,0:T(8,128)}, /*index=5*/f32[3,64,512]{2,1,0:T(8,128)}, f32[3,64,512]{2,1,0:T(8,128)}) custom-call(f32[1024,1024]{1,0:T(8,128)} %get-tuple-element.70.args_0_, f32[1024,128]{1,0:T(8,128)} %fusion.2.args_1_, ...), custom_call_target="tpu_custom_call" | custom-call | flops 28991029248 | bytes 62914560 | tf_op jit(solution)/shard_map/backward/pallas_call | solution.py:822
  446.1 0.0 copy-start.3
  446.1 0.0 copy-start.5
  446.1 0.0 copy-start.2
  446.2 0.0 copy-start.4
  446.2 0.0 copy-start.7
  446.2 0.0 copy-start.1
  446.2 2.2 maximum_bitcast_fusion
  448.4 0.0 copy-done.6
  448.4 1.6 pad_maximum_fusion.2
  450.0 0.0 copy-done.3
  450.0 0.0 copy-done.5
  450.0 0.8 pad_maximum_fusion
  450.9 0.0 copy-done.2
  450.9 0.0 copy-done.4
  450.9 0.8 pad_maximum_fusion.1
  451.7 0.0 copy-done.7
  451.7 0.7 constant_dynamic-slice_fusion.1
  452.4 0.0 copy-done.1
  452.4 0.0 copy-start
  452.4 1.3 copy.19
  453.7 1.6 copy-done
  455.3 2.0 copy.20
  (1 shorter events, 0.0 us)
Async XLA Ops:
  324.5 123.9 %copy-start.6 = (f32[64,512]{1,0:T(8,128)S(1)}, f32[64,512]{1,0:T(8,128)}, u32[]{:S(2)}) copy-start(f32[64,512]{1,0:T(8,128)} %get-tuple-element.92) | copy-start | bytes 393220
  446.1 3.9 copy-start.3
  446.1 3.9 copy-start.5
  446.1 4.7 %copy-start.2 = (f32[64,1024]{1,0:T(8,128)S(1)}, f32[64,1024]{1,0:T(8,128)}, u32[]{:S(2)}) copy-start(f32[64,1024]{1,0:T(8,128)} %get-tuple-element.96) | copy-start | bytes 786436
  446.2 4.7 %copy-start.4 = (f32[64,1024]{1,0:T(8,128)S(1)}, f32[64,1024]{1,0:T(8,128)}, u32[]{:S(2)}) copy-start(f32[64,1024]{1,0:T(8,128)} %get-tuple-element.95) | copy-start | bytes 786436
  446.2 5.6 %copy-start.7 = (f32[8,128]{1,0:T(8,128)S(1)}, f32[8,128]{1,0:T(8,128)}, u32[]{:S(2)}) copy-start(f32[8,128]{1,0:T(8,128)} %get-tuple-element.97) | copy-start | bytes 12292
  446.2 6.2 %copy-start.1 = (bf16[1024,1024]{1,0:T(8,128)(2,1)S(1)}, bf16[1024,1024]{1,0:T(8,128)(2,1)}, u32[]{:S(2)}) copy-start(bf16[1024,1024]{1,0:T(8,128)(2,1)} %get-tuple-element.114) | copy-start | bytes 6291460
  452.4 2.9 copy-start
